TPU v7x, 512 devices: a whole 4x8x8 slice. The times are simulated.
512 devices in a mesh: seq: 32 (over y, z_lo, core), row: 4 (over x), col: 4 (over z_hi).
Axes of the slice: x: 4, y: 8, z: 8 (z_hi: 4, z_lo: 2; z = z_hi * 2 + z_lo), core: 2. Of those that a mesh axis runs over, the one named last changes fastest.
Arguments:
- hidden_in: bfloat16 [4, 16384, 1024], P('row', 'seq')
- qkv_weight: bfloat16 [1024, 16, 192], P(None, 'col'), may hold values from -0.1875 to 0.1875
- qkv_global_weight: bfloat16 [1024, 16, 192], P('row', 'col'), may hold values from -0.1875 to 0.1875
- out_weight: bfloat16 [1024, 1024], P('col'), may hold values from -0.75 to 0.75
- ln_gain: float32 [1024], replicated, may hold values from 0.1 to 1.9
- ln_bias: float32 [1024], replicated, may hold values from -3 to 3
- ffn_in: bfloat16 [1024, 4096], P('row', 'col'), may hold values from -0.1875 to 0.1875
- ffn_out: bfloat16 [4096, 1024], P('col', 'row'), may hold values from -0.09375 to 0.09375
- ln2_gain: float32 [1024], replicated, may hold values from 0.1 to 1.9
- ln2_bias: float32 [1024], replicated, may hold values from -3 to 3
- segment_ids: int32 [4, 16384], P('row'), may hold values from 0 to 63, never falling along the last dimension, each value on 1 to 9216 neighbouring positions
- global_pos: int32 [4, 128], P('row'), may hold values from 0 to 16383, as said below
- page_owner: int32 [4, 1024, 1], P('row', 'seq'), may hold values from 0 to 31; in each aligned block of 32 rows (0 to 31, 32 to 63, ..., all dimensions but the last counted through in order) at most 2 rows name the same one
Outputs:
- hidden_out: bfloat16 [4, 16384, 1024], P('row', ('seq', 'col'))
- page_pool: bfloat16 [4, 32, 32, 2, 16, 16, 128], P('row', 'seq', None, None, None, 'col')
Inputs may be any that keep to these rules, and one draw needn't show every extreme that they name: `segment_ids`: in each stream, prompt numbers never fall along positions and every prompt has 1 to 9216 tokens, one exactly 9216. `global_pos`: in each stream, exactly 4 distinct global positions lie in each block of 512 consecutive tokens, listed in increasing order. `page_owner`: among the 32 pages of one shard of a stream, at most 2 have the same owner.
All inputs are finite; a program needn't handle non-finite values.
Results may differ from a plain program's by a relative error of at most 0.014.
The roundings to bfloat16 on the way count: a program that leaves them out, or rounds other values in their place, can miss the bound.
Values may be sent and summed in bfloat16 or wider, within the bound.
A program may use at most 64 MiB of HBM per device.

v0:
```python
import math
import jax
import jax.numpy as jnp
from jax import lax
from jax.sharding import PartitionSpec as P

HALF = 256


def padded(block, sides, width):
    for axis, dim in sides:
        count = lax.axis_size(axis)
        forward = [(i, i + 1) for i in range(count - 1)]
        backward = [(target, source) for source, target in forward]
        low = lax.ppermute(
            lax.slice_in_dim(block, block.shape[dim] - width, None, axis=dim), axis, forward
        )
        high = lax.ppermute(lax.slice_in_dim(block, 0, width, axis=dim), axis, backward)
        block = jnp.concatenate([low, block, high], axis=dim)
    return block


def layer_norm(values, gain, bias):
    center = values - jnp.mean(values, axis=1, keepdims=True)
    spread = jnp.mean(center * center, axis=1, keepdims=True)
    return center * lax.rsqrt(spread + 1e-05) * gain + bias


def per_device(
    hidden_in,
    qkv_weight,
    qkv_global_weight,
    out_weight,
    ln_gain,
    ln_bias,
    ffn_in,
    ffn_out,
    ln2_gain,
    ln2_bias,
    segment_ids,
    global_pos,
    page_owner,
):
    neg = -1e30
    tokens = hidden_in[0]
    shard_len, width = tokens.shape
    heads_here = qkv_weight.shape[1]
    triple = qkv_weight.shape[2]
    head_dim = triple // 3
    n_seq = lax.axis_size("seq")
    n_row = lax.axis_size("row")
    n_col = lax.axis_size("col")
    seq_index = lax.axis_index("seq")
    col_index = lax.axis_index("col")
    base = seq_index * shard_len
    scale = 1.0 / math.sqrt(head_dim)
    all_pos = global_pos[0]
    n_glob = all_pos.shape[0]
    per_shard = n_glob // n_seq
    own_pos = lax.dynamic_slice_in_dim(all_pos, seq_index * per_shard, per_shard, 0)
    local_order = jnp.arange(shard_len, dtype=jnp.int32)
    own_match = (own_pos - base)[:, None] == local_order[None, :]
    picker = own_match.astype(jnp.bfloat16)
    own_rows = jnp.dot(picker, tokens, preferred_element_type=jnp.float32).astype(jnp.bfloat16)
    glob_rows = lax.all_gather(own_rows, "seq", axis=0, tiled=True)
    wg_rows = qkv_global_weight.shape[0]
    fi_rows, units = ffn_in.shape
    wg_flat = qkv_global_weight.reshape(-1)
    fi_flat = ffn_in.reshape(-1)
    fo_flat = ffn_out.reshape(-1)
    n_wg, n_fi = (wg_flat.shape[0], fi_flat.shape[0])
    everything = lax.all_gather(jnp.concatenate([wg_flat, fi_flat, fo_flat]), "row", axis=0)
    w_global = everything[:, :n_wg].reshape(n_row * wg_rows, heads_here * triple)
    f_in = everything[:, n_wg : n_wg + n_fi].reshape(n_row * fi_rows, units)
    f_out = jnp.transpose(
        everything[:, n_wg + n_fi :].reshape(n_row, units, ffn_out.shape[1]), (1, 0, 2)
    ).reshape(units, n_row * ffn_out.shape[1])
    w_out = lax.all_gather(out_weight, "col", axis=0, tiled=True)
    flat_weight = qkv_weight.reshape(width, heads_here * triple)
    qkv = jnp.dot(tokens, flat_weight, preferred_element_type=jnp.float32).astype(jnp.bfloat16)
    qkv_heads = qkv.reshape(shard_len, heads_here, triple)
    queries = qkv_heads[:, :, :head_dim]
    kv_local = qkv_heads[:, :, head_dim:]
    owners = page_owner[0, :, 0]
    n_pages = owners.shape[0]
    page_len = shard_len // n_pages
    capacity = max(2, n_pages // n_seq)
    page_order = jnp.arange(n_pages, dtype=jnp.int32)
    slot = jnp.sum(
        ((owners[:, None] == owners[None, :]) & (page_order[None, :] < page_order[:, None])).astype(
            jnp.int32
        ),
        axis=1,
    )
    target = owners * capacity + slot
    placing = (target[None, :] == jnp.arange(n_seq * capacity, dtype=jnp.int32)[:, None]).astype(
        jnp.bfloat16
    )
    outgoing = jnp.dot(
        placing,
        kv_local.reshape(n_pages, page_len * heads_here * 2 * head_dim),
        preferred_element_type=jnp.float32,
    ).astype(jnp.bfloat16)
    outgoing = outgoing.reshape(n_seq, capacity, page_len, heads_here, 2 * head_dim)
    arrived = lax.all_to_all(outgoing, "seq", split_axis=0, concat_axis=0, tiled=True)
    page_pool = arrived[None, None]
    kv_ext = padded(kv_local, (("seq", 0),), HALF)
    glob_qkv = jnp.dot(glob_rows, flat_weight, preferred_element_type=jnp.float32).astype(
        jnp.bfloat16
    )
    glob_kv = glob_qkv.reshape(n_glob, heads_here, triple)[:, :, head_dim:]
    glob_k = glob_kv[:, :, :head_dim]
    glob_v = glob_kv[:, :, head_dim:]
    glob_q = (
        jnp.dot(glob_rows, w_global, preferred_element_type=jnp.float32)
        .astype(jnp.bfloat16)
        .reshape(n_glob, heads_here, triple)[:, :, :head_dim]
    )
    global_kv_local = (
        jnp.dot(tokens, w_global, preferred_element_type=jnp.float32)
        .astype(jnp.bfloat16)
        .reshape(shard_len, heads_here, triple)[:, :, head_dim:]
    )
    seg_all = segment_ids[0]
    glob_seg = jnp.take(seg_all, all_pos)
    seg_pad = jnp.pad(seg_all, (HALF, HALF), constant_values=-1)
    query_seg = lax.dynamic_slice_in_dim(seg_all, base, shard_len, 0)
    key_seg = lax.dynamic_slice_in_dim(seg_pad, base, shard_len + 2 * HALF, 0)
    key_pos = base - HALF + jnp.arange(shard_len + 2 * HALF, dtype=jnp.int32)
    key_flag = jnp.any(key_pos[:, None] == all_pos[None, :], axis=1)
    query_pos = base + local_order
    s_part = (
        jnp.einsum(
            "ghd,khd->hgk",
            glob_q,
            global_kv_local[:, :, :head_dim],
            preferred_element_type=jnp.float32,
        )
        * scale
    )
    part_mask = glob_seg[:, None] == query_seg[None, :]
    part_top = jnp.max(jnp.where(part_mask, s_part, neg), axis=2)
    glob_top = lax.pmax(part_top, "seq")
    e_part = jnp.where(part_mask, jnp.exp(s_part - glob_top[:, :, None]), 0.0)
    part_total = jnp.sum(e_part, axis=2)
    part_acc = jnp.einsum(
        "hgk,khd->hgd",
        e_part,
        global_kv_local[:, :, head_dim:].astype(jnp.float32),
        precision=lax.Precision.HIGHEST,
    )
    summed = lax.psum(jnp.concatenate([part_acc, part_total[:, :, None]], axis=2), "seq")
    glob_out = (summed[:, :, :head_dim] / summed[:, :, head_dim:]).astype(jnp.bfloat16)
    glob_mask = query_seg[:, None] == glob_seg[None, :]
    k_blk = kv_ext[:, :, :head_dim]
    v_blk = kv_ext[:, :, head_dim:]
    s_win = jnp.einsum("qhd,khd->hqk", queries, k_blk, preferred_element_type=jnp.float32) * scale
    s_glob = jnp.einsum("qhd,ghd->hqg", queries, glob_k, preferred_element_type=jnp.float32) * scale
    m_win = (
        (jnp.abs(query_pos[:, None] - key_pos[None, :]) <= HALF)
        & (query_seg[:, None] == key_seg[None, :])
        & jnp.logical_not(key_flag[None, :])
    )
    top = jnp.maximum(
        jnp.max(jnp.where(m_win, s_win, neg), axis=2),
        jnp.max(jnp.where(glob_mask, s_glob, neg), axis=2),
    )
    e_win = jnp.where(m_win, jnp.exp(s_win - top[:, :, None]), 0.0)
    e_glob = jnp.where(glob_mask, jnp.exp(s_glob - top[:, :, None]), 0.0)
    total = jnp.sum(e_win, axis=2) + jnp.sum(e_glob, axis=2)
    numer = jnp.einsum(
        "hqk,khd->qhd", e_win.astype(jnp.bfloat16), v_blk, preferred_element_type=jnp.float32
    )
    numer = numer + jnp.einsum(
        "hqg,ghd->qhd", e_glob.astype(jnp.bfloat16), glob_v, preferred_element_type=jnp.float32
    )
    pieces = (numer / jnp.transpose(total)[:, :, None]).astype(jnp.bfloat16)
    own_out = lax.dynamic_slice_in_dim(glob_out, seq_index * per_shard, per_shard, 1)
    placed = jnp.einsum("gt,hgd->thd", picker, own_out, preferred_element_type=jnp.float32).astype(
        jnp.bfloat16
    )
    is_own = jnp.any(own_match, axis=0)
    attention = jnp.where(is_own[:, None, None], placed, pieces).reshape(
        shard_len, heads_here * head_dim
    )
    attn_all = lax.all_gather(attention, "col", axis=0)
    attn_full = jnp.transpose(attn_all, (1, 0, 2)).reshape(shard_len, n_col * heads_here * head_dim)
    proj = jnp.dot(attn_full, w_out, preferred_element_type=jnp.float32)
    middle = layer_norm(tokens.astype(jnp.float32) + proj, ln_gain, ln_bias).astype(jnp.bfloat16)
    ffn_pre = jnp.dot(middle, f_in, preferred_element_type=jnp.float32)
    ffn_hidden = jax.nn.gelu(ffn_pre, approximate=False).astype(jnp.bfloat16)
    ffn_part = lax.psum_scatter(
        jnp.dot(ffn_hidden, f_out, preferred_element_type=jnp.float32),
        "col",
        scatter_dimension=0,
        tiled=True,
    )
    out_rows = shard_len // n_col
    mine = lax.dynamic_slice_in_dim(middle, col_index * out_rows, out_rows, 0).astype(jnp.float32)
    normed = layer_norm(mine + ffn_part, ln2_gain, ln2_bias)
    return (normed.astype(jnp.bfloat16)[None], page_pool)


def solution(mesh):
    in_specs = (
        P("row", "seq", None),
        P(None, "col", None),
        P("row", "col", None),
        P("col", None),
        P(),
        P(),
        P("row", "col"),
        P("col", "row"),
        P(),
        P(),
        P("row", None),
        P("row", None),
        P("row", "seq", None),
    )
    out_specs = (P("row", ("seq", "col"), None), P("row", "seq", None, None, None, "col", None))
    return jax.shard_map(
        per_device, mesh=mesh, in_specs=in_specs, out_specs=out_specs, check_vma=False
    )
```

profile of v0, /device:TPU:1, one launch (start us, length us, event | category | flops | bytes accessed | tf_op | source)
XLA Modules:
  0.0 554.5 jit_solution(4400960408158859480)
XLA Ops:
  12.9 1.9 convolution_convert_fusion.1
  17.1 5.4 collective-permute-start
  22.5 5.4 collective-permute-start.1
  28.3 32.6 %all-gather.1 = bf16[32,4,1024]{2,1,0:T(4,128)(2,1)S(1)} all-gather(bf16[1,4,1024]{2,1,0:T(4,128)(2,1)S(1)} %fusion.24), channel_id=1, replica_groups=mesh['seq'=32,'row'=4,'col'=4] {'seq'}, dimensions={0}, use_global_device_ids=true | all-gather | bytes 270336 | tf_op jit(solution)/shard_map/all_gather | solution.py:65
  69.9 2.7 fusion
  72.8 2.0 fusion.70
  74.8 9.9 %all-gather.10.cloned.1.call-done = bf16[2883584]{0:T(1024)(128)(2,1)} async-done(((bf16[720896]{0:T(1024)(128)(2,1)}), bf16[2883584]{0:T(1024)(128)(2,1)}) %all-gather.10.cloned.1.call-update) | async-done | bytes 5767184 | tf_op jit(solution)/shard_map/all_gather | solution.py:72
  84.7 7.2 %reshape.195 = bf16[4,720896]{1,0:T(4,128)(2,1)} reshape(bf16[2883584]{0:T(1024)(128)(2,1)} %all-gather.10.cloned.1.call-done) | data formatting | bytes 11534336 | tf_op jit(solution)/shard_map/all_gather | solution.py:72
  95.1 3.2 convolution_convert_fusion.2
  100.0 53.4 %pmax.7 = f32[4,128]{1,0:T(4,128)S(1)} all-reduce(f32[4,128]{1,0:T(4,128)S(1)} %get-tuple-element.10), channel_id=1, replica_groups=mesh['seq'=32,'row'=4,'col'=4] {'seq'}, use_global_device_ids=true, to_apply=%region_2.3 | all-reduce | flops 512 | bytes 4096 | tf_op jit(solution)/shard_map/pmax | solution.py:143
  153.5 1.9 fusion.67
  156.5 5.3 fusion.63
  161.8 205.0 %all-reduce.3.cloned.1.call-done = f32[4,128,65]{1,2,0:T(8,128)} async-done(((f32[4,128,65]{1,2,0:T(8,128)}), f32[4,128,65]{1,2,0:T(8,128)}) %all-reduce.3.cloned.1.call-update) | async-done | bytes 133136 | tf_op jit(solution)/shard_map/psum | solution.py:152
  370.3 4.0 fusion.139
  375.9 4.0 copy.66
  379.9 4.8 reshape.182
  384.7 23.1 %all-gather.6.cloned.1.call-done = bf16[4,512,256]{2,1,0:T(8,128)(2,1)} async-done(((bf16[1,512,256]{2,1,0:T(8,128)(2,1)}), bf16[4,512,256]{2,1,0:T(8,128)(2,1)}) %all-gather.6.cloned.1.call-update) | async-done | bytes 1048592 | tf_op jit(solution)/shard_map/all_gather | solution.py:186
  409.5 53.6 %all-gather.8.cloned.1.call-done = bf16[1024,1024]{1,0:T(8,128)(2,1)} async-done(((bf16[256,1024]{1,0:T(8,128)(2,1)}), bf16[1024,1024]{1,0:T(8,128)(2,1)}) %all-gather.8.cloned.1.call-update) | async-done | bytes 2097168 | tf_op jit(solution)/shard_map/all_gather | solution.py:78
  463.1 2.9 fusion.141
  468.1 9.8 %fusion.25 = f32[512,1024]{1,0:T(8,128)} fusion(bf16[1024,1024]{0,1:T(8,128)(2,1)} %bitcast.92, bf16[512,1024]{1,0:T(8,128)(2,1)S(1)} %add_convert_fusion, bf16[1024,1024]{1,0:T(8,128)(2,1)} %reshape.182), kind=kOutput, calls=%fused_computation.47 | convolution fusion | flops 2181562368 | bytes 7340032 | tf_op jit(solution)/shard_map/dot_general | solution.py:193
  481.9 9.3 %all-to-all-start = ((bf16[32,2,16,4,128]{4,3,2,1,0:T(4,128)(2,1)}), bf16[32,2,16,4,128]{4,3,2,1,0:T(4,128)(2,1)S(1)}, u32[]{:S(2)}, u32[]{:S(2)}) async-start(bf16[32,2,16,4,128]{4,3,2,1,0:T(4,128)(2,1)} %reshape.186), calls=%async_computation.1 | async-start | bytes 2097152 | tf_op jit(solution)/shard_map/all_to_all | solution.py:105
  491.1 28.1 %all-to-all-done = bf16[32,2,16,4,128]{4,3,2,1,0:T(4,128)(2,1)S(1)} async-done(((bf16[32,2,16,4,128]{4,3,2,1,0:T(4,128)(2,1)}), bf16[32,2,16,4,128]{4,3,2,1,0:T(4,128)(2,1)S(1)}, u32[]{:S(2)}, u32[]{:S(2)}) %all-to-all-start) | async-done | bytes 1048608 | tf_op jit(solution)/shard_map/all_to_all | solution.py:105
  519.3 23.1 %reduce-scatter.2.cloned.1.call-done = f32[128,1024]{1,0:T(8,128)} async-done(((f32[512,1024]{1,0:T(8,128)}), f32[128,1024]{1,0:T(8,128)}) %reduce-scatter.2.cloned.1.call-update) | async-done | bytes 524304 | tf_op jit(solution)/shard_map/reduce_scatter | solution.py:192
  545.0 2.0 fusion.81
  (121 shorter events, 39.8 us)
Async XLA Ops:
  7.2 5.3 copy-start
  7.2 3.1 copy-start.14
  7.2 3.1 copy-start.15
  7.2 77.5 %all-gather.10.cloned.1.call-start = ((), (), s32[]{:S(2)}) async-start(), calls=%async_computation.6 | async-start | bytes 7208960 | tf_op jit(solution)/shard_map/all_gather | solution.py:72
  12.4 354.4 %all-reduce.3.cloned.1.call-start = ((), (), s32[]{:S(2)}) async-start(), calls=%async_computation.2 | async-start | bytes 294912 | tf_op jit(solution)/shard_map/psum | solution.py:152
  14.8 13.1 %copy-start.21 = (s32[1,128]{1,0:T(1,128)S(1)}, s32[1,128]{1,0:T(1,128)}, u32[]{:S(2)}) copy-start(s32[1,128]{1,0:T(1,128)} %param.24) | copy-start | bytes 1540
  14.9 46.1 %copy-start.3 = (s32[1,16384]{1,0:T(1,128)S(1)}, s32[1,16384]{1,0:T(1,128)}, u32[]{:S(2)}) copy-start(s32[1,16384]{1,0:T(1,128)} %param.23) | copy-start | bytes 196612
  17.1 49.5 %collective-permute-start = (bf16[256,4,128]{0,2,1:T(8,128)(2,1)}, bf16[256,4,128]{0,2,1:T(8,128)(2,1)}, u32[]{:S(2)}, u32[]{:S(2)}) collective-permute-start(bf16[256,4,128]{0,2,1:T(8,128)(2,1)} %get-tuple-element.4), channel_id=1, source_target_pairs={{0,16},{16,32},{32,48},{48,64},{64,80},{80,96},{96,112},{112,128},... | collective-permute-start | bytes 786440 | tf_op jit(solution)/shard_map/ppermute | solution.py:15
  22.5 44.2 %collective-permute-start.1 = (bf16[256,4,128]{0,2,1:T(8,128)(2,1)}, bf16[256,4,128]{0,2,1:T(8,128)(2,1)}, u32[]{:S(2)}, u32[]{:S(2)}) collective-permute-start(bf16[256,4,128]{0,2,1:T(8,128)(2,1)} %get-tuple-element.5), channel_id=1, source_target_pairs={{16,0},{32,16},{48,32},{64,48},{80,64},{96,80},{112,96},{128,112},... | collective-permute-start | bytes 786440 | tf_op jit(solution)/shard_map/ppermute | solution.py:18
  63.7 6.1 %copy-start.9 = (pred[512,1024]{1,0:T(8,128)(4,1)}, pred[512,1024]{1,0:T(8,128)(4,1)S(1)}, u32[]{:S(2)}) copy-start(pred[512,1024]{1,0:T(8,128)(4,1)S(1)} %fusion.15) | copy-start | bytes 1572868
  64.5 5.0 copy-start.4
  69.6 3.2 copy-start.2
  98.5 58.0 %copy-start.10 = (pred[512,1024]{1,0:T(8,128)(4,1)S(1)}, pred[512,1024]{1,0:T(8,128)(4,1)}, u32[]{:S(2)}) copy-start(pred[512,1024]{1,0:T(8,128)(4,1)} %copy-done.9) | copy-start | bytes 1572868
  98.5 58.0 %copy-start.13 = (bf16[1024,4,128]{0,2,1:T(8,128)(2,1)S(1)}, bf16[1024,4,128]{0,2,1:T(8,128)(2,1)}, u32[]{:S(2)}) copy-start(bf16[1024,4,128]{0,2,1:T(8,128)(2,1)} %copy-done.12) | copy-start | bytes 3145732
  98.5 58.0 %copy-start.16 = (f32[4,64,512]{2,1,0:T(8,128)S(1)}, f32[4,64,512]{2,1,0:T(8,128)}, u32[]{:S(2)}) copy-start(f32[4,64,512]{2,1,0:T(8,128)} %fusion.70) | copy-start | bytes 1572868
  156.4 251.3 %all-gather.6.cloned.1.call-start = ((), (), s32[]{:S(2)}) async-start(), calls=%async_computation.3 | async-start | bytes 1310720 | tf_op jit(solution)/shard_map/all_gather | solution.py:186
  369.7 93.4 %all-gather.8.cloned.1.call-start = ((), (), s32[]{:S(2)}) async-start(), calls=%async_computation.4 | async-start | bytes 2621440 | tf_op jit(solution)/shard_map/all_gather | solution.py:78
  370.3 172.1 %reduce-scatter.2.cloned.1.call-start = ((), (), s32[]{:S(2)}) async-start(), calls=%async_computation.5 | async-start | bytes 2621440 | tf_op jit(solution)/shard_map/reduce_scatter | solution.py:192
  384.7 78.4 %copy-start.7 = (bf16[1,512,1024]{2,1,0:T(8,128)(2,1)S(1)}, bf16[1,512,1024]{2,1,0:T(8,128)(2,1)}, u32[]{:S(2)}) copy-start(bf16[1,512,1024]{2,1,0:T(8,128)(2,1)} %param.13) | copy-start | bytes 3145732
  477.9 1.8 copy-start.22
  481.8 63.2 %copy-start.19 = (f32[1024]{0:T(1024)S(1)}, f32[1024]{0:T(1024)}, u32[]{:S(2)}) copy-start(f32[1024]{0:T(1024)} %param.22) | copy-start | bytes 12292
  481.9 63.2 %copy-start.20 = (f32[1024]{0:T(1024)S(1)}, f32[1024]{0:T(1024)}, u32[]{:S(2)}) copy-start(f32[1024]{0:T(1024)} %param.21) | copy-start | bytes 12292
  481.9 37.4 %all-to-all-start = ((bf16[32,2,16,4,128]{4,3,2,1,0:T(4,128)(2,1)}), bf16[32,2,16,4,128]{4,3,2,1,0:T(4,128)(2,1)S(1)}, u32[]{:S(2)}, u32[]{:S(2)}) async-start(bf16[32,2,16,4,128]{4,3,2,1,0:T(4,128)(2,1)} %reshape.186), calls=%async_computation.1 | async-start | bytes 2097152 | tf_op jit(solution)/shard_map/all_to_all | solution.py:105
  542.3 5.7 %copy-start.1 = (bf16[1024,4,192]{0,2,1:T(8,128)(2,1)S(1)}, bf16[1024,4,192]{0,2,1:T(8,128)(2,1)}, u32[]{:S(2)}) copy-start(bf16[1024,4,192]{0,2,1:T(8,128)(2,1)} %param.14) | copy-start | bytes 4718596
  (8 other events, 9.3 us)
Sparse Core Ops, SparseCore 0:
  12.6 72.0 all-gather.9
  156.6 210.2 all-reduce.2
  369.8 37.9 all-gather.5
  409.9 53.1 all-gather.7
  478.1 64.2 reduce-scatter.1
where the time goes:
time: 556 us; the launch traced here: 555 us
  waiting for transfers between devices  343 us (62%)
  blocking collectives  86.1 us (15%)
  local copies, waits for them, and re-layouts  43.5 us (8%)
  matrix products  33.5 us (6%)
  starting transfers between devices  20.2 us (4%)
  between operations  14.3 us (3%)
  other arithmetic  13.6 us (2%)
    psum x1, waiting for transfers between devices, per_device(): lax.psum(jnp.concatenate([part_acc, part_total[:, :, None]], axis=2), 'seq')  205 us
    all_gather x1, waiting for transfers between devices, per_device(): w_out = lax.all_gather(out_weight, 'col', axis=0, tiled=True)  53.6 us
    pmax x1, blocking collectives, per_device(): glob_top = lax.pmax(part_top, 'seq')  53.4 us
    all_gather x1, blocking collectives, per_device(): glob_rows = lax.all_gather(own_rows, 'seq', axis=0, tiled=True)  32.6 us
    all_to_all x1, waiting for transfers between devices, per_device(): lax.all_to_all(outgoing, 'seq', split_axis=0, concat_axis=0, tiled=True)  28.1 us
    reduce_scatter x1, waiting for transfers between devices, per_device(): lax.psum_scatter(jnp.dot(ffn_hidden, f_out, preferred_element_type=jnp.fl...  23.1 us
    all_gather x1, waiting for transfers between devices, per_device(): attn_all = lax.all_gather(attention, 'col', axis=0)  23.1 us
  transfers between devices with their start and end apart: 8, of which 6 were waited for; matrix products, arithmetic and copies ran while one was open for 8% of the time, Pallas kernels for 0%

commit v1 on v0

--- a/solution.py
+++ b/solution.py
@@ -149,7 +149,9 @@
         global_kv_local[:, :, head_dim:].astype(jnp.float32),
         precision=lax.Precision.HIGHEST,
     )
-    summed = lax.psum(jnp.concatenate([part_acc, part_total[:, :, None]], axis=2), "seq")
+    summed = jnp.sum(
+        lax.all_gather(jnp.concatenate([part_acc, part_total[:, :, None]], axis=2), "seq"), axis=0
+    )
     glob_out = (summed[:, :, :head_dim] / summed[:, :, head_dim:]).astype(jnp.bfloat16)
     glob_mask = query_seg[:, None] == glob_seg[None, :]
     k_blk = kv_ext[:, :, :head_dim]

time: 556 us -> 415 us (0.75)
  waiting for transfers between devices: 343 us -> 206 us
    psum x1 -> x0, waiting for transfers between devices: 205 us -> none  [per_device(): lax.psum(jnp.concatenate([part_acc, part_total[:, :, None]], axis=2), 'seq')]
    all_gather x0 -> x1, waiting for transfers between devices: none -> 48.6 us  [per_device(): lax.all_gather(jnp.concatenate([part_acc, part_total[:, :, None]], axis=2...]
    all_gather x1, waiting for transfers between devices: 9.93 us -> 32.3 us  [per_device(): lax.all_gather(jnp.concatenate([wg_flat, fi_flat, fo_flat]), 'row', axis=0)]
  transfers between devices with their start and end apart: 8 -> 8, of which waited for: 6 -> 7; matrix products, arithmetic and copies ran while one was open for 8% -> 9% of each run, Pallas kernels for 0% -> 0%
where the time goes in v1:
time: 415 us; the launch traced here: 414 us
  waiting for transfers between devices  206 us (50%)
  blocking collectives  91 us (22%)
  local copies, waits for them, and re-layouts  39 us (9%)
  matrix products  30 us (7%)
  starting transfers between devices  17.4 us (4%)
  other arithmetic  16.2 us (4%)
  between operations  14.2 us (3%)
    all_gather x1, waiting for transfers between devices, per_device(): w_out = lax.all_gather(out_weight, 'col', axis=0, tiled=True)  53.4 us
    pmax x1, blocking collectives, per_device(): glob_top = lax.pmax(part_top, 'seq')  53.2 us
    all_gather x1, waiting for transfers between devices, per_device(): lax.all_gather(jnp.concatenate([part_acc, part_total[:, :, None]], axis=2...  48.6 us
    all_gather x1, blocking collectives, per_device(): glob_rows = lax.all_gather(own_rows, 'seq', axis=0, tiled=True)  37.8 us
    all_gather x1, waiting for transfers between devices, per_device(): lax.all_gather(jnp.concatenate([wg_flat, fi_flat, fo_flat]), 'row', axis=0)  32.3 us
    all_to_all x1, waiting for transfers between devices, per_device(): lax.all_to_all(outgoing, 'seq', split_axis=0, concat_axis=0, tiled=True)  28.3 us
    reduce_scatter x1, waiting for transfers between devices, per_device(): lax.psum_scatter(jnp.dot(ffn_hidden, f_out, preferred_element_type=jnp.fl...  22.1 us
    all_gather x1, waiting for transfers between devices, per_device(): attn_all = lax.all_gather(attention, 'col', axis=0)  20.8 us
  transfers between devices with their start and end apart: 8, of which 7 were waited for; matrix products, arithmetic and copies ran while one was open for 9% of the time, Pallas kernels for 0%

profile of v1, /device:TPU:1, one launch (start us, length us, event | category | flops | bytes accessed | tf_op | source)
XLA Modules:
  0.0 414.1 jit_solution(10061713030474531043)
XLA Ops:
  12.0 37.8 %all-gather.2 = bf16[32,4,1024]{2,1,0:T(4,128)(2,1)S(1)} all-gather(bf16[1,4,1024]{2,1,0:T(4,128)(2,1)S(1)} %fusion.24), channel_id=1, replica_groups=mesh['seq'=32,'row'=4,'col'=4] {'seq'}, dimensions={0}, use_global_device_ids=true | all-gather | bytes 270336 | tf_op jit(solution)/shard_map/all_gather | solution.py:65
  51.2 32.3 %all-gather.12.cloned.1.call-done = bf16[2883584]{0:T(1024)(128)(2,1)} async-done(((bf16[720896]{0:T(1024)(128)(2,1)}), bf16[2883584]{0:T(1024)(128)(2,1)}) %all-gather.12.cloned.1.call-update) | async-done | bytes 5767184 | tf_op jit(solution)/shard_map/all_gather | solution.py:72
  83.6 7.2 %reshape.195 = bf16[4,720896]{1,0:T(4,128)(2,1)} reshape(bf16[2883584]{0:T(1024)(128)(2,1)} %all-gather.12.cloned.1.call-done) | data formatting | bytes 11534336 | tf_op jit(solution)/shard_map/all_gather | solution.py:72
  92.2 2.6 reshape.175
  94.8 3.7 convolution_convert_fusion.2
  99.1 2.4 select_reduce_fusion.2
  101.5 53.2 %pmax.7 = f32[4,128]{1,0:T(4,128)S(1)} all-reduce(f32[4,128]{1,0:T(4,128)S(1)} %get-tuple-element.10), channel_id=1, replica_groups=mesh['seq'=32,'row'=4,'col'=4] {'seq'}, use_global_device_ids=true, to_apply=%region_2.3 | all-reduce | flops 512 | bytes 4096 | tf_op jit(solution)/shard_map/pmax | solution.py:143
  154.7 2.3 fusion.67
  162.3 3.0 collective-permute-start
  165.3 4.9 %collective-permute-start.1 = (bf16[256,4,128]{0,2,1:T(8,128)(2,1)}, bf16[256,4,128]{0,2,1:T(8,128)(2,1)}, u32[]{:S(2)}, u32[]{:S(2)}) collective-permute-start(bf16[256,4,128]{0,2,1:T(8,128)(2,1)} %get-tuple-element.5), channel_id=1, source_target_pairs={{16,0},{32,16},{48,32},{64,48},{80,64},{96,80},{112,96},{128,112},... | collective-permute-start | bytes 786440 | tf_op jit(solution)/shard_map/ppermute | solution.py:18
  176.4 2.7 fusion
  179.4 2.1 fusion.63
  181.5 48.6 %all-gather.14.cloned.1.call-done = f32[128,128,65]{1,2,0:T(8,128)} async-done(((f32[4,128,65]{1,2,0:T(8,128)}), f32[128,128,65]{1,2,0:T(8,128)}) %all-gather.14.cloned.1.call-update) | async-done | bytes 4259856 | tf_op jit(solution)/shard_map/all_gather | solution.py:153
  230.1 2.6 reduce_sum.82
  234.8 4.0 fusion.136
  240.4 4.0 copy.63
  244.4 4.8 %reshape.182 = bf16[1024,1024]{1,0:T(8,128)(2,1)} reshape(bf16[4,262144]{1,0:T(4,128)(2,1)} %get-tuple-element.2) | data formatting | bytes 4194304 | tf_op jit(solution)/shard_map/reshape | solution.py:74
  249.2 20.8 %all-gather.8.cloned.1.call-done = bf16[4,512,256]{2,1,0:T(8,128)(2,1)} async-done(((bf16[1,512,256]{2,1,0:T(8,128)(2,1)}), bf16[4,512,256]{2,1,0:T(8,128)(2,1)}) %all-gather.8.cloned.1.call-update) | async-done | bytes 1048592 | tf_op jit(solution)/shard_map/all_gather | solution.py:188
  271.7 53.4 %all-gather.10.cloned.1.call-done = bf16[1024,1024]{1,0:T(8,128)(2,1)} async-done(((bf16[256,1024]{1,0:T(8,128)(2,1)}), bf16[1024,1024]{1,0:T(8,128)(2,1)}) %all-gather.10.cloned.1.call-update) | async-done | bytes 2097168 | tf_op jit(solution)/shard_map/all_gather | solution.py:78
  325.1 2.9 fusion.138
  329.2 10.2 %fusion.25 = f32[512,1024]{1,0:T(8,128)} fusion(bf16[1024,1024]{0,1:T(8,128)(2,1)} %bitcast.94, bf16[512,1024]{1,0:T(8,128)(2,1)S(1)} %add_convert_fusion, bf16[1024,1024]{1,0:T(8,128)(2,1)} %reshape.182), kind=kOutput, calls=%fused_computation.47 | convolution fusion | flops 2181562368 | bytes 7340032 | tf_op jit(solution)/shard_map/dot_general | solution.py:195
  342.2 9.3 %all-to-all-start = ((bf16[32,2,16,4,128]{4,3,2,1,0:T(4,128)(2,1)}), bf16[32,2,16,4,128]{4,3,2,1,0:T(4,128)(2,1)S(1)}, u32[]{:S(2)}, u32[]{:S(2)}) async-start(bf16[32,2,16,4,128]{4,3,2,1,0:T(4,128)(2,1)} %reshape.186), calls=%async_computation.1 | async-start | bytes 2097152 | tf_op jit(solution)/shard_map/all_to_all | solution.py:105
  351.5 28.3 %all-to-all-done = bf16[32,2,16,4,128]{4,3,2,1,0:T(4,128)(2,1)S(1)} async-done(((bf16[32,2,16,4,128]{4,3,2,1,0:T(4,128)(2,1)}), bf16[32,2,16,4,128]{4,3,2,1,0:T(4,128)(2,1)S(1)}, u32[]{:S(2)}, u32[]{:S(2)}) %all-to-all-start) | async-done | bytes 1048608 | tf_op jit(solution)/shard_map/all_to_all | solution.py:105
  379.8 22.1 %reduce-scatter.2.cloned.1.call-done = f32[128,1024]{1,0:T(8,128)} async-done(((f32[512,1024]{1,0:T(8,128)}), f32[128,1024]{1,0:T(8,128)}) %reduce-scatter.2.cloned.1.call-update) | async-done | bytes 524304 | tf_op jit(solution)/shard_map/reduce_scatter | solution.py:194
  (112 shorter events, 34.7 us)
Async XLA Ops:
  7.2 151.0 %copy-start = (bf16[1024,4,192]{0,2,1:T(8,128)(2,1)S(1)}, bf16[1024,4,192]{0,2,1:T(8,128)(2,1)}, u32[]{:S(2)}) copy-start(bf16[1024,4,192]{0,2,1:T(8,128)(2,1)} %param.14) | copy-start | bytes 4718596
  7.2 2.3 copy-start.9
  7.2 2.4 copy-start.10
  7.2 76.4 %all-gather.12.cloned.1.call-start = ((), (), s32[]{:S(2)}) async-start(), calls=%async_computation.5 | async-start | bytes 7208960 | tf_op jit(solution)/shard_map/all_gather | solution.py:72
  10.0 1.3 copy-start.15
  10.0 1.7 copy-start.4
  11.3 38.7 %copy-start.3 = (s32[1,16384]{1,0:T(1,128)S(1)}, s32[1,16384]{1,0:T(1,128)}, u32[]{:S(2)}) copy-start(s32[1,16384]{1,0:T(1,128)} %param.23) | copy-start | bytes 196612
  11.3 218.8 %all-gather.14.cloned.1.call-start = ((), (), s32[]{:S(2)}) async-start(), calls=%async_computation.6 | async-start | bytes 4866048 | tf_op jit(solution)/shard_map/all_gather | solution.py:153
  90.8 1.4 slice-start
  94.8 3.7 copy-start.2
  99.1 59.0 %copy-start.5 = (bf16[1,512,1024]{2,1,0:T(8,128)(2,1)S(1)}, bf16[1,512,1024]{2,1,0:T(8,128)(2,1)}, u32[]{:S(2)}) copy-start(bf16[1,512,1024]{2,1,0:T(8,128)(2,1)} %param.13) | copy-start | bytes 3145732
  154.7 2.3 copy-start.8
  158.1 111.9 %all-gather.8.cloned.1.call-start = ((), (), s32[]{:S(2)}) async-start(), calls=%async_computation.2 | async-start | bytes 1310720 | tf_op jit(solution)/shard_map/all_gather | solution.py:188
  162.3 10.7 %collective-permute-start = (bf16[256,4,128]{0,2,1:T(8,128)(2,1)}, bf16[256,4,128]{0,2,1:T(8,128)(2,1)}, u32[]{:S(2)}, u32[]{:S(2)}) collective-permute-start(bf16[256,4,128]{0,2,1:T(8,128)(2,1)} %get-tuple-element.4), channel_id=1, source_target_pairs={{0,16},{16,32},{32,48},{48,64},{64,80},{80,96},{96,112},{112,128},... | collective-permute-start | bytes 786440 | tf_op jit(solution)/shard_map/ppermute | solution.py:15
  165.3 8.0 %collective-permute-start.1 = (bf16[256,4,128]{0,2,1:T(8,128)(2,1)}, bf16[256,4,128]{0,2,1:T(8,128)(2,1)}, u32[]{:S(2)}, u32[]{:S(2)}) collective-permute-start(bf16[256,4,128]{0,2,1:T(8,128)(2,1)} %get-tuple-element.5), channel_id=1, source_target_pairs={{16,0},{32,16},{48,32},{64,48},{80,64},{96,80},{112,96},{128,112},... | collective-permute-start | bytes 786440 | tf_op jit(solution)/shard_map/ppermute | solution.py:18
  234.2 90.9 %all-gather.10.cloned.1.call-start = ((), (), s32[]{:S(2)}) async-start(), calls=%async_computation.3 | async-start | bytes 2621440 | tf_op jit(solution)/shard_map/all_gather | solution.py:78
  234.8 167.2 %reduce-scatter.2.cloned.1.call-start = ((), (), s32[]{:S(2)}) async-start(), calls=%async_computation.4 | async-start | bytes 2621440 | tf_op jit(solution)/shard_map/reduce_scatter | solution.py:194
  249.2 75.9 %copy-start.6 = (bf16[1,512,1024]{2,1,0:T(8,128)(2,1)S(1)}, bf16[1,512,1024]{2,1,0:T(8,128)(2,1)}, u32[]{:S(2)}) copy-start(bf16[1,512,1024]{2,1,0:T(8,128)(2,1)} %param.13) | copy-start | bytes 3145732
  329.1 10.2 %copy-start.7 = (bf16[512,1024]{1,0:T(8,128)(2,1)}, bf16[512,1024]{1,0:T(8,128)(2,1)S(1)}, u32[]{:S(2)}) copy-start(bf16[512,1024]{1,0:T(8,128)(2,1)S(1)} %add_convert_fusion) | copy-start | bytes 3145732
  339.3 0.7 copy-start.16
  342.2 62.4 %copy-start.13 = (f32[1024]{0:T(1024)S(1)}, f32[1024]{0:T(1024)}, u32[]{:S(2)}) copy-start(f32[1024]{0:T(1024)} %param.22) | copy-start | bytes 12292
  342.2 62.4 %copy-start.14 = (f32[1024]{0:T(1024)S(1)}, f32[1024]{0:T(1024)}, u32[]{:S(2)}) copy-start(f32[1024]{0:T(1024)} %param.21) | copy-start | bytes 12292
  342.2 37.6 %all-to-all-start = ((bf16[32,2,16,4,128]{4,3,2,1,0:T(4,128)(2,1)}), bf16[32,2,16,4,128]{4,3,2,1,0:T(4,128)(2,1)S(1)}, u32[]{:S(2)}, u32[]{:S(2)}) async-start(bf16[32,2,16,4,128]{4,3,2,1,0:T(4,128)(2,1)} %reshape.186), calls=%async_computation.1 | async-start | bytes 2097152 | tf_op jit(solution)/shard_map/all_to_all | solution.py:105
  401.9 5.7 %copy-start.1 = (bf16[1024,4,192]{0,2,1:T(8,128)(2,1)S(1)}, bf16[1024,4,192]{0,2,1:T(8,128)(2,1)}, u32[]{:S(2)}) copy-start(bf16[1024,4,192]{0,2,1:T(8,128)(2,1)} %param.14) | copy-start | bytes 4718596
  (2 other events, 1.4 us)
Sparse Core Ops, SparseCore 0:
  11.4 72.0 all-gather.11
  158.2 71.8 all-gather.13
  234.3 35.6 all-gather.7
  271.9 53.1 all-gather.9
  339.5 62.4 reduce-scatter.1
